TPU v7x, 256 devices: a whole 4x4x8 slice. The times are simulated.
256 devices in a mesh: cuts: 128 (over y, z, x), site: 2 (over core).
Axes of the slice: x: 4, y: 4, z: 8, core: 2. Of those that a mesh axis runs over, the one named last changes fastest.
Arguments:
- field: float32 [128, 2048], P('cuts'), may hold values from -4 to 4
- momenta: float32 [128, 2048], P('cuts'), may hold values from -4 to 4
- start_force: float32 [128, 2048], P('cuts'), may hold values from -4 to 4
- green: bfloat16 [128, 2048, 2048], P('cuts', 'site'), as said below
- forward_prop: bfloat16 [2048, 2048], P('site')
- back_prop: bfloat16 [2048, 2048], P('site')
- accept: int32 [128], P('cuts'), may hold values from 0 to 1
Outputs:
- new_field: float32 [128, 2048], P('cuts')
- new_momenta: float32 [128, 2048], P('cuts')
- new_force: float32 [128, 2048], P('cuts')
- energy_change: float32 [1], replicated
Inputs may be any that keep to these rules, and one draw needn't show every extreme that they name: green has a diagonal of 0.2 to 0.8 plus full-rank off-diagonal entries; the propagators are the identity plus full-rank entries.
All inputs are finite; a program needn't handle non-finite values.
Results may differ from a plain program's by a relative error of at most 0.0029.
Values may be sent and summed in bfloat16 or wider, within the bound.
No kernel may reach another device: no remote copies, remote signals or barrier semaphores. Data moves between devices by JAX's collectives and lax.ppermute only.
A program may use at most 128 MiB of HBM per device.

v0:
```python
import functools

import jax
import jax.numpy as jnp
from jax import lax
from jax.sharding import Mesh
from jax.sharding import PartitionSpec as P

CUTS = ("cuts_0", "cuts_1", "cuts_2")


coupling = 0.5
stepsize = 0.2


def from_behind(shard, axis, by):
    size = lax.axis_size(axis)
    return lax.ppermute(shard, axis, [(i, (i + by) % size) for i in range(size)])


def laid_out(tiles, dim):
    tiles = jnp.moveaxis(tiles, 0, dim)
    lengths = tiles.shape
    return tiles.reshape(*lengths[:dim], lengths[dim] * lengths[dim + 1], *lengths[dim + 2 :])


def sent_to_all(shard, axis):
    copies = jnp.broadcast_to(shard, (lax.axis_size(axis), *shard.shape))
    return lax.all_to_all(copies, axis, split_axis=0, concat_axis=0, tiled=True)


def gathered_copies(shard, axis, dim):
    return laid_out(sent_to_all(shard, axis), dim)


def by_axis(shard, axes):
    return functools.reduce(lax.psum, axes, shard)


def on_device(field, momenta, start_force, green, forward_prop, back_prop, accept):
    half = momenta - 0.5 * stepsize * start_force
    trial = field + stepsize * half
    start_local = jnp.sum(momenta * momenta) + jnp.sum(field * field)
    source = green[0]
    phase = from_behind(trial[0], CUTS, -1)
    rows = source.shape[0]
    row_start = lax.axis_index("site") * rows
    growth = jnp.exp(coupling * phase)
    row_growth = lax.dynamic_slice_in_dim(growth, row_start, rows)
    scaled = (row_growth[:, None] * source.astype(jnp.float32)).astype(jnp.bfloat16)
    wrapped = jnp.dot(
        forward_prop, gathered_copies(scaled, "site", 0), preferred_element_type=jnp.float32
    )
    shrink = jnp.exp(-coupling * phase)
    diag_part = jnp.sum(wrapped * (shrink[None, :] * back_prop.astype(jnp.float32)), axis=1)
    diag_part = from_behind(diag_part, CUTS, 1)
    diagonal = lax.all_gather(diag_part, "site", axis=0, tiled=True)
    new_force = trial - 2.0 * coupling * (1.0 - 2.0 * diagonal[None, :])
    new_momenta = half - 0.5 * stepsize * new_force
    end_local = jnp.sum(new_momenta * new_momenta) + jnp.sum(trial * trial)
    total = by_axis(end_local - start_local, CUTS)
    count = lax.axis_size(CUTS) * field.shape[0] * field.shape[1]
    change = total / (2.0 * jnp.sqrt(jnp.float32(count)))
    new_field = jnp.where(accept[0] == 1, trial, field)
    return (new_field, new_momenta, new_force, jnp.reshape(change, (1,)))


def solution(mesh):
    finer = Mesh(
        mesh.devices.reshape(4, 8, 4, mesh.shape["site"]), ("cuts_0", "cuts_1", "cuts_2", "site")
    )
    in_specs = (
        P(CUTS, None),
        P(CUTS, None),
        P(CUTS, None),
        P(CUTS, "site", None),
        P("site", None),
        P("site", None),
        P(CUTS),
    )
    out_specs = (P(CUTS, None), P(CUTS, None), P(CUTS, None), P())
    return jax.shard_map(
        on_device, mesh=finer, in_specs=in_specs, out_specs=out_specs, check_vma=False
    )
```

profile of v0, /device:TPU:42, one launch (start us, length us, event | category | flops | bytes accessed | tf_op | source)
XLA Modules:
  0.0 102.2 jit_solution(12920418493354641477)
XLA Ops:
  0.6 1.4 %multiply_reduce_fusion.2 = (f32[]{:T(128)}, f32[1,2048]{1,0:T(1,128)S(1)}, f32[]{:T(128)}, f32[]{:T(128)}) fusion(f32[1,2048]{1,0:T(1,128)} %param.7, f32[1,2048]{1,0:T(1,128)} %param.8, f32[1,2048]{1,0:T(1,128)} %param.9), kind=kLoop, calls=%fused_computation.7 | loop fusion | flops 20477 | bytes 32780 | tf_op jit(solution)/shard_map/reduce_sum | solution.py:60
  2.0 0.5 collective-permute-start
  2.5 6.4 %copy.12 = bf16[1024,2048]{0,1:T(8,128)(2,1)} copy(bf16[1024,2048]{1,0:T(8,128)(2,1)} %param.12) | data formatting | bytes 8388608 | tf_op args[5]
  8.9 0.0 collective-permute-done
  8.9 2.9 %fusion = bf16[1024,2048]{1,0:T(8,128)(2,1)S(1)} fusion(bf16[1,1024,2048]{2,1,0:T(8,128)(2,1)} %param.10, f32[1024]{0:T(1024)S(1)} %fusion.2), kind=kLoop, calls=%fused_computation.1 | loop fusion | flops 6291456 | bytes 8392704 | tf_op jit(solution)/shard_map/convert_element_type | solution.py:50
  11.9 4.3 %broadcast_in_dim.2 = bf16[2,1024,2048]{2,1,0:T(8,128)(2,1)} broadcast(bf16[1024,2048]{1,0:T(8,128)(2,1)S(1)} %fusion), dimensions={1,2} | broadcast | bytes 12582912 | tf_op jit(solution)/shard_map/broadcast_in_dim | solution.py:28
  16.2 6.9 %all-to-all-start = ((bf16[2,1024,2048]{2,1,0:T(8,128)(2,1)}), bf16[2,1024,2048]{2,1,0:T(8,128)(2,1)}, u32[]{:S(2)}, u32[]{:S(2)}) async-start(bf16[2,1024,2048]{2,1,0:T(8,128)(2,1)} %broadcast_in_dim.2), calls=%async_computation | async-start | bytes 16777216 | tf_op jit(solution)/shard_map/all_to_all | solution.py:29
  23.1 7.5 %all-to-all-done = bf16[2,1024,2048]{2,1,0:T(8,128)(2,1)} async-done(((bf16[2,1024,2048]{2,1,0:T(8,128)(2,1)}), bf16[2,1024,2048]{2,1,0:T(8,128)(2,1)}, u32[]{:S(2)}, u32[]{:S(2)}) %all-to-all-start) | async-done | bytes 8388640 | tf_op jit(solution)/shard_map/all_to_all | solution.py:29
  30.6 0.0 copy-start
  30.6 0.0 copy-start.1
  30.6 0.0 copy-start.2
  30.6 14.1 %fusion.1 = f32[1024]{0:T(1024)S(1)} fusion(bf16[1024,2048]{0,1:T(8,128)(2,1)} %copy.12, f32[2048]{0:T(1024)S(1)} %multiply_exponential_fusion, bf16[2048,2048]{1,0:T(8,128)(2,1)} %bitcast.3, bf16[1024,2048]{1,0:T(8,128)(2,1)} %param.11), kind=kOutput, calls=%fused_computation.3 | convolution fusion | flops 8598322176 | bytes 16789504 | tf_op jit(solution)/shard_map/dot_general | solution.py:51
  44.7 1.6 %collective-permute-start.1 = (f32[1024]{0:T(1024)S(1)}, f32[1024]{0:T(1024)S(1)}, u32[]{:S(2)}, u32[]{:S(2)}) collective-permute-start(f32[1024]{0:T(1024)S(1)} %fusion.1), channel_id=1, source_target_pairs={{0,2},{2,4},{4,6},{6,8},{8,10},{10,12},{12,14},{14,16},{16,18},{18... | collective-permute-start | bytes 12296 | tf_op jit(solution)/shard_map/ppermute | solution.py:18
  48.2 0.5 collective-permute-done.1
  48.7 1.8 %all_gather.3 = f32[2048]{0:T(1024)S(1)} all-gather(f32[1024]{0:T(1024)S(1)} %collective-permute-done.1), channel_id=1, replica_groups=mesh['cuts_0'=4,'cuts_1'=8,'cuts_2'=4,'site'=2] {'site'}, dimensions={0}, use_global_device_ids=true | all-gather | bytes 12288 | tf_op jit(solution)/shard_map/all_gather | solution.py:57
  50.5 0.0 copy-done
  50.5 0.0 copy-done.1
  50.5 0.0 copy-done.2
  50.5 1.2 %multiply_reduce_fusion.3 = (f32[]{:T(128)}, f32[1,2048]{1,0:T(1,128)}, f32[1,2048]{1,0:T(1,128)}, f32[1,2048]{1,0:T(1,128)}) fusion(f32[1,2048]{1,0:T(1,128)S(1)} %copy-done, f32[1,2048]{1,0:T(1,128)S(1)} %copy-done.1, f32[1,2048]{1,0:T(1,128)S(1)} %get-tuple-element.5, f32[1,2048]{1,0:T(1,128)S(1)} %bitcast.14, f32[1,2048]{1,0:T(1,128)S(1)} %copy-done.2, ...), kind=kLoop, calls=%fused_computation.8 | loop fusion | flops 16383 | bytes 65541 | tf_op jit(solution)/shard_map/reduce_sum | solution.py:60
  52.9 9.2 %psum.21 = f32[]{:T(128)} all-reduce(f32[]{:T(128)S(6)} %sub.27), channel_id=1, replica_groups=mesh['cuts_0'=4,'cuts_1'=8,'cuts_2'=4,'site'=2] {'cuts_0'}, use_global_device_ids=true, to_apply=%region_5.0 | all-reduce | flops 1 | bytes 8 | tf_op jit(solution)/shard_map/psum | solution.py:37
  62.2 22.5 %psum.22 = f32[]{:T(128)} all-reduce(f32[]{:T(128)} %psum.21), channel_id=1, replica_groups=mesh['cuts_0'=4,'cuts_1'=8,'cuts_2'=4,'site'=2] {'cuts_1'}, use_global_device_ids=true, to_apply=%region_6.0 | all-reduce | flops 1 | bytes 8 | tf_op jit(solution)/shard_map/psum | solution.py:37
  84.7 15.8 %psum.23 = f32[]{:T(128)} all-reduce(f32[]{:T(128)} %psum.22), channel_id=1, replica_groups=mesh['cuts_0'=4,'cuts_1'=8,'cuts_2'=4,'site'=2] {'cuts_2'}, use_global_device_ids=true, to_apply=%region_7.0 | all-reduce | flops 1 | bytes 8 | tf_op jit(solution)/shard_map/psum | solution.py:37
  (3 shorter events, 0.0 us)
Async XLA Ops:
  2.0 6.9 %collective-permute-start = (f32[2048]{0:T(1024)S(1)}, f32[2048]{0:T(1024)S(1)}, u32[]{:S(2)}, u32[]{:S(2)}) collective-permute-start(f32[2048]{0:T(1024)S(1)} %bitcast.15), channel_id=1, source_target_pairs={{0,254},{2,0},{4,2},{6,4},{8,6},{10,8},{12,10},{14,12},{16,14},{18... | collective-permute-start | bytes 24584 | tf_op jit(solution)/shard_map/ppermute | solution.py:18
  16.2 14.4 %all-to-all-start = ((bf16[2,1024,2048]{2,1,0:T(8,128)(2,1)}), bf16[2,1024,2048]{2,1,0:T(8,128)(2,1)}, u32[]{:S(2)}, u32[]{:S(2)}) async-start(bf16[2,1024,2048]{2,1,0:T(8,128)(2,1)} %broadcast_in_dim.2), calls=%async_computation | async-start | bytes 16777216 | tf_op jit(solution)/shard_map/all_to_all | solution.py:29
  30.6 19.9 %copy-start = (f32[1,2048]{1,0:T(1,128)S(1)}, f32[1,2048]{1,0:T(1,128)}, u32[]{:S(2)}) copy-start(f32[1,2048]{1,0:T(1,128)} %param.8) | copy-start | bytes 24580
  30.6 19.9 %copy-start.1 = (f32[1,2048]{1,0:T(1,128)S(1)}, f32[1,2048]{1,0:T(1,128)}, u32[]{:S(2)}) copy-start(f32[1,2048]{1,0:T(1,128)} %param.9) | copy-start | bytes 24580
  30.6 19.9 %copy-start.2 = (f32[1,2048]{1,0:T(1,128)S(1)}, f32[1,2048]{1,0:T(1,128)}, u32[]{:S(2)}) copy-start(f32[1,2048]{1,0:T(1,128)} %param.7) | copy-start | bytes 24580
  44.7 4.0 %collective-permute-start.1 = (f32[1024]{0:T(1024)S(1)}, f32[1024]{0:T(1024)S(1)}, u32[]{:S(2)}, u32[]{:S(2)}) collective-permute-start(f32[1024]{0:T(1024)S(1)} %fusion.1), channel_id=1, source_target_pairs={{0,2},{2,4},{4,6},{6,8},{8,10},{10,12},{12,14},{14,16},{16,18},{18... | collective-permute-start | bytes 12296 | tf_op jit(solution)/shard_map/ppermute | solution.py:18
where the time goes:
time: 103 us; the launch traced here: 102 us
  blocking collectives  49.3 us (48%)
  matrix products  14.1 us (14%)
  local copies, waits for them, and re-layouts  10.7 us (10%)
  starting transfers between devices  9.02 us (9%)
  waiting for transfers between devices  7.92 us (8%)
  between operations  5.64 us (5%)
  other arithmetic  5.55 us (5%)
    psum x3, blocking collectives, by_axis(): return functools.reduce(lax.psum, axes, shard)  47.5 us
    dot_general x1, matrix products, on_device(): jnp.dot(forward_prop, gathered_copies(scaled, 'site', 0), preferred_eleme...  14.1 us
    all_to_all x1, waiting for transfers between devices, sent_to_all(): return lax.all_to_all(copies, axis, split_axis=0, concat_axis=0, tiled=True)  7.47 us
    all_to_all x1, starting transfers between devices, sent_to_all(): return lax.all_to_all(copies, axis, split_axis=0, concat_axis=0, tiled=True)  6.92 us
    unnamed x7, local copies, waits for them, and re-layouts  6.41 us
    broadcast_in_dim x1, local copies, waits for them, and re-layouts, sent_to_all(): copies = jnp.broadcast_to(shard, (lax.axis_size(axis), *shard.shape))  4.27 us
    convert_element_type x1, other arithmetic, on_device(): (row_growth[:, None] * source.astype(jnp.float32)).astype(jnp.bfloat16)  2.93 us
    reduce_sum x2, other arithmetic, on_device(): end_local = jnp.sum(new_momenta * new_momenta) + jnp.sum(trial * trial)  2.6 us
  transfers between devices with their start and end apart: 3, of which 2 were waited for; matrix products, arithmetic and copies ran while one was open for 6% of the time, Pallas kernels for 0%

commit v1 on v0

v1 whole, which is shorter than its diff:
```python
import jax
import jax.numpy as jnp
from jax import lax
from jax.experimental import pallas as pl
from jax.experimental.pallas import tpu as pltpu
from jax.sharding import Mesh
from jax.sharding import PartitionSpec as P

CUTS = ("cuts_0", "cuts_1", "cuts_2")
ALL = (*CUTS, "site")
LANES = 128
COLUMNS = 256

coupling = 0.5
stepsize = 0.2


def stepped(field, momenta, start_force):
    half = momenta - 0.5 * stepsize * start_force
    return field + stepsize * half, half


def moved_by(trial, half, diagonal):
    force = trial - 2.0 * coupling * (1.0 - 2.0 * diagonal)
    return force, half - 0.5 * stepsize * force


def diagonal_kernel(nxt_ref, field_ref, momenta_ref, start_ref, near_ref, far_ref, forward_ref, back_ref,
                    diag_ref, part_ref, scaled, acc):
    rows, sites = forward_ref.shape
    blocks = rows // LANES
    site = lax.axis_index("site")
    first = site == 0

    def by_rows(row):
        whole = jnp.reshape(row, (2 * blocks, LANES))
        own = jnp.where(first, whole[:blocks], whole[blocks:])
        return own, jnp.where(first, whole[blocks:], whole[:blocks])

    growth = jnp.exp(coupling * nxt_ref[0:1, :])
    factors = jnp.transpose(jnp.concatenate(by_rows(growth), axis=0))
    near_at = pl.multiple_of(site * rows, LANES)
    far_at = pl.multiple_of((1 - site) * rows, LANES)

    def scale(j):
        span = pl.ds(j * COLUMNS, COLUMNS)
        for b in range(2 * blocks):
            source = near_ref if b < blocks else far_ref
            block = source[pl.ds(b % blocks * LANES, LANES), span].astype(jnp.float32)
            scaled[j % 2, pl.ds(b * LANES, LANES), :] = (factors[:, b : b + 1] * block).astype(jnp.bfloat16)

    steps = sites // COLUMNS
    scale(0)
    for j in range(steps):
        span = pl.ds(j * COLUMNS, COLUMNS)
        if j + 1 < steps:
            scale(j + 1)
        shrink = jnp.exp(-coupling * nxt_ref[0:1, span])
        wrapped = jnp.dot(
            forward_ref[:, pl.ds(near_at, rows)], scaled[j % 2, :rows, :], preferred_element_type=jnp.float32
        ) + jnp.dot(
            forward_ref[:, pl.ds(far_at, rows)], scaled[j % 2, rows:, :], preferred_element_type=jnp.float32
        )
        product = wrapped * (shrink * back_ref[:, span].astype(jnp.float32))
        part = product[:, :LANES] + product[:, LANES:]
        if j == 0:
            acc[...] = part
        else:
            acc[...] += part
    diag = jnp.concatenate(
        [
            jnp.sum(jnp.transpose(acc[pl.ds(b * LANES, LANES), :]), axis=0, keepdims=True)
            for b in range(blocks)
        ],
        axis=0,
    )
    diag_ref[...] = diag
    moved = moved_by(by_rows(nxt_ref[0:1, :])[0], by_rows(nxt_ref[1:2, :])[0], diag)[1]
    field, momenta = field_ref[...], momenta_ref[...]
    trial = stepped(field, momenta, start_ref[...])[0]
    total = jnp.sum(moved * moved) + 0.5 * jnp.sum(trial * trial - momenta * momenta - field * field)
    part_ref[...] = jnp.full(part_ref.shape, total, jnp.float32)


def closing_kernel(scale, accept_ref, field_ref, momenta_ref, start_ref, straight_ref, crossed_ref, parts_ref,
                   new_field_ref, new_momenta_ref, new_force_ref, change_ref):
    first = lax.axis_index("site") == 0
    straight, crossed = straight_ref[...], crossed_ref[...]
    diagonal = jnp.concatenate(
        [jnp.where(first, straight, crossed), jnp.where(first, crossed, straight)], axis=0
    )
    field = field_ref[...]
    trial, half = stepped(field, momenta_ref[...], start_ref[...])
    force, moved = moved_by(trial, half, jnp.reshape(diagonal, field.shape))
    new_force_ref[...] = force
    new_momenta_ref[...] = moved
    new_field_ref[...] = jnp.where(accept_ref[0] == 1, trial, field)
    change_ref[0] = scale * jnp.sum(parts_ref[...])


def on_device(field, momenta, start_force, green, forward_prop, back_prop, accept):
    near = green[0]
    rows, sites = near.shape
    devices = lax.axis_size(ALL)
    cuts = lax.axis_size(CUTS)
    row = jax.ShapeDtypeStruct((1, sites), jnp.float32)
    vmem = pl.BlockSpec(memory_space=pltpu.VMEM)
    smem = pl.BlockSpec(memory_space=pltpu.SMEM)

    def held(x):
        return pltpu.with_memory_space_constraint(x, pltpu.VMEM)

    far = lax.ppermute(near, "site", [(0, 1), (1, 0)])
    nxt = lax.ppermute(
        jnp.concatenate(stepped(field, momenta, start_force), axis=0),
        CUTS,
        [(i, (i - 1) % cuts) for i in range(cuts)],
    )
    diag, part = pl.pallas_call(
        diagonal_kernel,
        out_shape=(
            jax.ShapeDtypeStruct((rows // LANES, LANES), jnp.float32),
            jax.ShapeDtypeStruct((devices, LANES), jnp.float32),
        ),
        in_specs=[vmem] * 8,
        out_specs=(vmem, vmem),
        scratch_shapes=[
            pltpu.VMEM((2, sites, COLUMNS), jnp.bfloat16),
            pltpu.VMEM((rows, LANES), jnp.float32),
        ],
        compiler_params=pltpu.CompilerParams(vmem_limit_bytes=32 * 1024 * 1024),
        cost_estimate=pl.CostEstimate(
            flops=2 * rows * sites * sites, bytes_accessed=8 * rows * sites, transcendentals=2 * sites
        ),
        name="diagonal",
    )(*map(held, (nxt, field, momenta, start_force, near, far, forward_prop, back_prop)))
    straight = lax.ppermute(diag, ALL, [(i, (i + 2) % devices) for i in range(devices)])
    crossed = lax.ppermute(diag, ALL, [(i, ((i + 2) % devices) ^ 1) for i in range(devices)])
    parts = lax.all_to_all(part, ALL, split_axis=0, concat_axis=0, tiled=True)
    scale = 1.0 / (2.0 * (cuts * sites) ** 0.5) / LANES
    new_field, new_momenta, new_force, change = pl.pallas_call(
        lambda *refs: closing_kernel(scale, *refs),
        out_shape=(row, row, row, jax.ShapeDtypeStruct((1,), jnp.float32)),
        in_specs=[smem] + [vmem] * 6,
        out_specs=(vmem, vmem, vmem, smem),
        compiler_params=pltpu.CompilerParams(vmem_limit_bytes=4 * 1024 * 1024),
        name="closing",
    )(accept, *map(held, (field, momenta, start_force, straight, crossed, parts)))
    return new_field, new_momenta, new_force, change


def solution(mesh):
    finer = Mesh(
        mesh.devices.reshape(4, 8, 4, mesh.shape["site"]), ("cuts_0", "cuts_1", "cuts_2", "site")
    )
    in_specs = (
        P(CUTS, None),
        P(CUTS, None),
        P(CUTS, None),
        P(CUTS, "site", None),
        P("site", None),
        P("site", None),
        P(CUTS),
    )
    out_specs = (P(CUTS, None), P(CUTS, None), P(CUTS, None), P())
    return jax.shard_map(
        on_device, mesh=finer, in_specs=in_specs, out_specs=out_specs, check_vma=False
    )
```

time: 103 us -> 57.5 us (0.56)
  the two profiles are of different devices: /device:TPU:42 before, /device:TPU:1 now
where the time goes in v1:
time: 57.5 us; the launch traced here: 57.1 us
  starting transfers between devices  25.5 us (44%)
  Pallas kernels  10.9 us (19%)
  waiting for transfers between devices  9.9 us (17%)
  local copies, waits for them, and re-layouts  8.67 us (15%)
  between operations  1.34 us (2%)
  other arithmetic  0.77 us (1%)
    all_to_all x1, starting transfers between devices, on_device(): parts = lax.all_to_all(part, ALL, split_axis=0, concat_axis=0, tiled=True)  10.5 us
    pallas_call x1, Pallas kernels, on_device(): pl.pallas_call(diagonal_kernel, out_shape=(jax.ShapeDtypeStruct((rows //...  10.2 us
    unnamed x18, local copies, waits for them, and re-layouts  8.67 us
    ppermute x1, starting transfers between devices, on_device(): lax.ppermute(jnp.concatenate(stepped(field, momenta, start_force), axis=0...  8.59 us
    ppermute x1, waiting for transfers between devices, on_device(): lax.ppermute(diag, ALL, [(i, (i + 2) % devices) for i in range(devices)])  7 us
    ppermute x1, starting transfers between devices, on_device(): far = lax.ppermute(near, 'site', [(0, 1), (1, 0)])  3.29 us
    ppermute x1, starting transfers between devices, on_device(): lax.ppermute(diag, ALL, [(i, (i + 2) % devices ^ 1) for i in range(device...  1.74 us
    all_to_all x1, waiting for transfers between devices, on_device(): parts = lax.all_to_all(part, ALL, split_axis=0, concat_axis=0, tiled=True)  1.47 us
  transfers between devices with their start and end apart: 5, of which 4 were waited for; matrix products, arithmetic and copies ran while one was open for 1% of the time, Pallas kernels for 0%

profile of v1, /device:TPU:1, one launch (start us, length us, event | category | flops | bytes accessed | tf_op | source)
XLA Modules:
  0.0 57.1 jit_solution(3001548274775927511)
XLA Ops:
  0.6 3.3 %collective-permute-start.1 = (bf16[1024,2048]{1,0:T(8,128)(2,1)}, bf16[1024,2048]{1,0:T(8,128)(2,1)S(1)}, u32[]{:S(2)}, u32[]{:S(2)}) collective-permute-start(bf16[1024,2048]{1,0:T(8,128)(2,1)} %bitcast.6), channel_id=1, source_target_pairs={{0,1},{1,0},{2,3},{3,2},{4,5},{5,4},{6,7},{7,6},{8,9},{9,8},{10,11... | collective-permute-start | bytes 12582920 | tf_op jit(solution)/shard_map/ppermute | solution.py:113
  3.9 0.8 %multiply_add_fusion = (f32[1,2048]{1,0:T(1,128)S(1)}, f32[1,2048]{1,0:T(1,128)S(1)}) fusion(f32[1,2048]{1,0:T(1,128)} %refs_1_.1, f32[1,2048]{1,0:T(1,128)} %refs_2_.1, f32[1,2048]{1,0:T(1,128)} %refs_3_.1), kind=kLoop, calls=%fused_computation.1 | loop fusion | flops 8192 | bytes 40960 | tf_op jit(solution)/shard_map/add | solution.py:20
  4.7 0.0 copy-start.1
  4.7 0.0 copy-start.3
  4.7 0.0 copy-start.5
  4.7 8.6 %collective-permute-start = (f32[2,2048]{1,0:T(2,128)S(1)}, f32[2,2048]{1,0:T(2,128)S(1)}, u32[]{:S(2)}, u32[]{:S(2)}) collective-permute-start(f32[2,2048]{1,0:T(2,128)S(1)} %pad_maximum_fusion), channel_id=1, source_target_pairs={{0,254},{2,0},{4,2},{6,4},{8,6},{10,8},{12,10},{14,12},{16,14},{18... | collective-permute-start | bytes 49160 | tf_op jit(solution)/shard_map/ppermute | solution.py:114
  13.3 0.9 %collective-permute-done.nxt_ref = f32[2,2048]{1,0:T(2,128)S(1)} collective-permute-done((f32[2,2048]{1,0:T(2,128)S(1)}, f32[2,2048]{1,0:T(2,128)S(1)}, u32[]{:S(2)}, u32[]{:S(2)}) %collective-permute-start) | collective-permute-done | bytes 16416 | tf_op jit(solution)/shard_map/ppermute | solution.py:114
  14.2 0.0 collective-permute-done.1.far_ref
  14.2 0.0 copy-start
  14.2 0.7 %copy-done = f32[1,2048]{1,0:T(1,128)S(1)} copy-done((f32[1,2048]{1,0:T(1,128)S(1)}, f32[1,2048]{1,0:T(1,128)}, u32[]{:S(2)}) %copy-start) | copy-done | bytes 8216
  14.9 0.0 copy-start.2
  14.9 0.7 %copy-done.2 = f32[1,2048]{1,0:T(1,128)S(1)} copy-done((f32[1,2048]{1,0:T(1,128)S(1)}, f32[1,2048]{1,0:T(1,128)}, u32[]{:S(2)}) %copy-start.2) | copy-done | bytes 8216
  15.6 0.0 copy-start.4
  15.6 0.7 %copy-done.4 = f32[1,2048]{1,0:T(1,128)S(1)} copy-done((f32[1,2048]{1,0:T(1,128)S(1)}, f32[1,2048]{1,0:T(1,128)}, u32[]{:S(2)}) %copy-start.4) | copy-done | bytes 8216
  16.3 0.0 copy-start.6
  16.3 2.2 %copy-done.6 = bf16[1,1024,2048]{2,1,0:T(8,128)(2,1)S(1)} copy-done((bf16[1,1024,2048]{2,1,0:T(8,128)(2,1)S(1)}, bf16[1,1024,2048]{2,1,0:T(8,128)(2,1)}, u32[]{:S(2)}) %copy-start.6) | copy-done | bytes 4194328
  18.5 0.0 copy-start.7
  18.5 2.2 %copy-done.7 = bf16[1024,2048]{1,0:T(8,128)(2,1)S(1)} copy-done((bf16[1024,2048]{1,0:T(8,128)(2,1)S(1)}, bf16[1024,2048]{1,0:T(8,128)(2,1)}, u32[]{:S(2)}) %copy-start.7) | copy-done | bytes 4194328
  20.7 0.0 copy-start.8
  20.7 2.2 %copy-done.8 = bf16[1024,2048]{1,0:T(8,128)(2,1)S(1)} copy-done((bf16[1024,2048]{1,0:T(8,128)(2,1)S(1)}, bf16[1024,2048]{1,0:T(8,128)(2,1)}, u32[]{:S(2)}) %copy-start.8) | copy-done | bytes 4194328
  22.9 10.2 %diagonal.1 = (f32[8,128]{1,0:T(8,128)S(1)}, f32[256,128]{1,0:T(8,128)}) custom-call(f32[2,2048]{1,0:T(2,128)S(1)} %collective-permute-done.nxt_ref, f32[1,2048]{1,0:T(1,128)S(1)} %copy-done, f32[1,2048]{1,0:T(1,128)S(1)} %copy-done.2, f32[1,2048]{1,0:T(1,128)S(1)} %copy-done.4, bf16[1024,2048]{1,0:T(8,128)(2,1)S(1)} %bitcast.7, ...), custom_call_target="tpu_custom_call" | custom-call | flops 8589934592 | bytes 16777216 | tf_op jit(solution)/shard_map/diagonal/pallas_call | solution.py:119
  33.1 10.5 %all-to-all-start = ((f32[256,1,128]{2,1,0:T(1,128)}), f32[256,1,128]{2,1,0:T(1,128)S(1)}, u32[]{:S(2)}, u32[]{:S(2)}) async-start(f32[256,1,128]{2,1,0:T(1,128)} %bitcast.2), calls=%async_computation | async-start | bytes 262144 | tf_op jit(solution)/shard_map/all_to_all | solution.py:139
  43.6 1.4 %collective-permute-start.2 = (f32[8,128]{1,0:T(8,128)S(1)}, f32[8,128]{1,0:T(8,128)S(1)}, u32[]{:S(2)}, u32[]{:S(2)}) collective-permute-start(f32[8,128]{1,0:T(8,128)S(1)} %get-tuple-element.6), channel_id=1, source_target_pairs={{0,2},{1,3},{2,4},{3,5},{4,6},{5,7},{6,8},{7,9},{8,10},{9,11},{10,... | collective-permute-start | bytes 12296 | tf_op jit(solution)/shard_map/ppermute | solution.py:137
  45.0 1.7 %collective-permute-start.3 = (f32[8,128]{1,0:T(8,128)S(1)}, f32[8,128]{1,0:T(8,128)S(1)}, u32[]{:S(2)}, u32[]{:S(2)}) collective-permute-start(f32[8,128]{1,0:T(8,128)S(1)} %get-tuple-element.6), channel_id=1, source_target_pairs={{0,3},{1,2},{2,5},{3,4},{4,7},{5,6},{6,9},{7,8},{8,11},{9,10},{10,... | collective-permute-start | bytes 12296 | tf_op jit(solution)/shard_map/ppermute | solution.py:138
  47.4 7.0 %collective-permute-done.2.refs_4_ = f32[8,128]{1,0:T(8,128)S(1)} collective-permute-done((f32[8,128]{1,0:T(8,128)S(1)}, f32[8,128]{1,0:T(8,128)S(1)}, u32[]{:S(2)}, u32[]{:S(2)}) %collective-permute-start.2) | collective-permute-done | bytes 4128 | tf_op jit(solution)/shard_map/ppermute | solution.py:137
  54.4 0.6 collective-permute-done.3.refs_5_
  54.9 1.5 %all-to-all-done = f32[256,1,128]{2,1,0:T(1,128)S(1)} async-done(((f32[256,1,128]{2,1,0:T(1,128)}), f32[256,1,128]{2,1,0:T(1,128)S(1)}, u32[]{:S(2)}, u32[]{:S(2)}) %all-to-all-start) | async-done | bytes 131104 | tf_op jit(solution)/shard_map/all_to_all | solution.py:139
  56.4 0.0 copy-done.1
  56.4 0.0 copy-done.3
  56.4 0.0 copy-done.5
  56.4 0.7 %closing.1 = (f32[1,2048]{1,0:T(1,128)}, f32[1,2048]{1,0:T(1,128)}, f32[1,2048]{1,0:T(1,128)}, f32[1]{0:T(128)}) custom-call(s32[1]{0:T(128)S(6)} %copy.12.refs_0_, f32[1,2048]{1,0:T(1,128)S(1)} %copy-done.1, f32[1,2048]{1,0:T(1,128)S(1)} %copy-done.3, f32[1,2048]{1,0:T(1,128)S(1)} %copy-done.5, f32[8,128]{1,0:T(8,128)S(1)} %collective-permute-done.2.refs_4_, ...), custom_call_target="tpu_custom_call" | custom-call | tf_op jit(solution)/shard_map/closing/pallas_call | solution.py:141
  (1 shorter events, 0.0 us)
Async XLA Ops:
  0.6 13.6 %collective-permute-start.1 = (bf16[1024,2048]{1,0:T(8,128)(2,1)}, bf16[1024,2048]{1,0:T(8,128)(2,1)S(1)}, u32[]{:S(2)}, u32[]{:S(2)}) collective-permute-start(bf16[1024,2048]{1,0:T(8,128)(2,1)} %bitcast.6), channel_id=1, source_target_pairs={{0,1},{1,0},{2,3},{3,2},{4,5},{5,4},{6,7},{7,6},{8,9},{9,8},{10,11... | collective-permute-start | bytes 12582920 | tf_op jit(solution)/shard_map/ppermute | solution.py:113
  4.7 51.7 %copy-start.1 = (f32[1,2048]{1,0:T(1,128)S(1)}, f32[1,2048]{1,0:T(1,128)}, u32[]{:S(2)}) copy-start(f32[1,2048]{1,0:T(1,128)} %refs_1_.1) | copy-start | bytes 24580
  4.7 51.7 %copy-start.3 = (f32[1,2048]{1,0:T(1,128)S(1)}, f32[1,2048]{1,0:T(1,128)}, u32[]{:S(2)}) copy-start(f32[1,2048]{1,0:T(1,128)} %refs_2_.1) | copy-start | bytes 24580
  4.7 51.7 %copy-start.5 = (f32[1,2048]{1,0:T(1,128)S(1)}, f32[1,2048]{1,0:T(1,128)}, u32[]{:S(2)}) copy-start(f32[1,2048]{1,0:T(1,128)} %refs_3_.1) | copy-start | bytes 24580
  4.7 9.5 %collective-permute-start = (f32[2,2048]{1,0:T(2,128)S(1)}, f32[2,2048]{1,0:T(2,128)S(1)}, u32[]{:S(2)}, u32[]{:S(2)}) collective-permute-start(f32[2,2048]{1,0:T(2,128)S(1)} %pad_maximum_fusion), channel_id=1, source_target_pairs={{0,254},{2,0},{4,2},{6,4},{8,6},{10,8},{12,10},{14,12},{16,14},{18... | collective-permute-start | bytes 49160 | tf_op jit(solution)/shard_map/ppermute | solution.py:114
  14.2 0.7 %copy-start = (f32[1,2048]{1,0:T(1,128)S(1)}, f32[1,2048]{1,0:T(1,128)}, u32[]{:S(2)}) copy-start(f32[1,2048]{1,0:T(1,128)} %refs_1_.1) | copy-start | bytes 24580
  14.9 0.7 %copy-start.2 = (f32[1,2048]{1,0:T(1,128)S(1)}, f32[1,2048]{1,0:T(1,128)}, u32[]{:S(2)}) copy-start(f32[1,2048]{1,0:T(1,128)} %refs_2_.1) | copy-start | bytes 24580
  15.6 0.7 %copy-start.4 = (f32[1,2048]{1,0:T(1,128)S(1)}, f32[1,2048]{1,0:T(1,128)}, u32[]{:S(2)}) copy-start(f32[1,2048]{1,0:T(1,128)} %refs_3_.1) | copy-start | bytes 24580
  16.3 2.2 %copy-start.6 = (bf16[1,1024,2048]{2,1,0:T(8,128)(2,1)S(1)}, bf16[1,1024,2048]{2,1,0:T(8,128)(2,1)}, u32[]{:S(2)}) copy-start(bf16[1,1024,2048]{2,1,0:T(8,128)(2,1)} %param.10) | copy-start | bytes 12582916
  18.5 2.2 %copy-start.7 = (bf16[1024,2048]{1,0:T(8,128)(2,1)S(1)}, bf16[1024,2048]{1,0:T(8,128)(2,1)}, u32[]{:S(2)}) copy-start(bf16[1024,2048]{1,0:T(8,128)(2,1)} %forward_ref.1) | copy-start | bytes 12582916
  20.7 2.2 %copy-start.8 = (bf16[1024,2048]{1,0:T(8,128)(2,1)S(1)}, bf16[1024,2048]{1,0:T(8,128)(2,1)}, u32[]{:S(2)}) copy-start(bf16[1024,2048]{1,0:T(8,128)(2,1)} %back_ref.1) | copy-start | bytes 12582916
  33.1 23.3 %all-to-all-start = ((f32[256,1,128]{2,1,0:T(1,128)}), f32[256,1,128]{2,1,0:T(1,128)S(1)}, u32[]{:S(2)}, u32[]{:S(2)}) async-start(f32[256,1,128]{2,1,0:T(1,128)} %bitcast.2), calls=%async_computation | async-start | bytes 262144 | tf_op jit(solution)/shard_map/all_to_all | solution.py:139
  43.6 10.8 %collective-permute-start.2 = (f32[8,128]{1,0:T(8,128)S(1)}, f32[8,128]{1,0:T(8,128)S(1)}, u32[]{:S(2)}, u32[]{:S(2)}) collective-permute-start(f32[8,128]{1,0:T(8,128)S(1)} %get-tuple-element.6), channel_id=1, source_target_pairs={{0,2},{1,3},{2,4},{3,5},{4,6},{5,7},{6,8},{7,9},{8,10},{9,11},{10,... | collective-permute-start | bytes 12296 | tf_op jit(solution)/shard_map/ppermute | solution.py:137
  45.0 10.0 %collective-permute-start.3 = (f32[8,128]{1,0:T(8,128)S(1)}, f32[8,128]{1,0:T(8,128)S(1)}, u32[]{:S(2)}, u32[]{:S(2)}) collective-permute-start(f32[8,128]{1,0:T(8,128)S(1)} %get-tuple-element.6), channel_id=1, source_target_pairs={{0,3},{1,2},{2,5},{3,4},{4,7},{5,6},{6,9},{7,8},{8,11},{9,10},{10,... | collective-permute-start | bytes 12296 | tf_op jit(solution)/shard_map/ppermute | solution.py:138

commit v2 on v1

--- a/solution.py
+++ b/solution.py
@@ -25,7 +25,23 @@
     return force, half - 0.5 * stepsize * force
 
 
-def diagonal_kernel(nxt_ref, field_ref, momenta_ref, start_ref, near_ref, far_ref, forward_ref, back_ref,
+def opening_kernel(field_ref, momenta_ref, start_ref, sent_ref, own_ref, held, sems):
+    copies = [
+        pltpu.make_async_copy(ref, held.at[k], sems.at[k])
+        for k, ref in enumerate((field_ref, momenta_ref, start_ref))
+    ]
+    for copy in copies:
+        copy.start()
+    for copy in copies:
+        copy.wait()
+    field, momenta = held[0], held[1]
+    trial, half = stepped(field, momenta, held[2])
+    sent_ref[0:1, :] = trial
+    sent_ref[1:2, :] = half
+    own_ref[...] = trial * trial - momenta * momenta - field * field
+
+
+def diagonal_kernel(nxt_ref, own_ref, near_ref, far_ref, forward_ref, back_ref,
                     diag_ref, part_ref, scaled, acc):
     rows, sites = forward_ref.shape
     blocks = rows // LANES
@@ -76,9 +92,7 @@
     )
     diag_ref[...] = diag
     moved = moved_by(by_rows(nxt_ref[0:1, :])[0], by_rows(nxt_ref[1:2, :])[0], diag)[1]
-    field, momenta = field_ref[...], momenta_ref[...]
-    trial = stepped(field, momenta, start_ref[...])[0]
-    total = jnp.sum(moved * moved) + 0.5 * jnp.sum(trial * trial - momenta * momenta - field * field)
+    total = jnp.sum(moved * moved) + 0.5 * jnp.sum(own_ref[...])
     part_ref[...] = jnp.full(part_ref.shape, total, jnp.float32)
 
 
@@ -111,18 +125,24 @@
         return pltpu.with_memory_space_constraint(x, pltpu.VMEM)
 
     far = lax.ppermute(near, "site", [(0, 1), (1, 0)])
-    nxt = lax.ppermute(
-        jnp.concatenate(stepped(field, momenta, start_force), axis=0),
-        CUTS,
-        [(i, (i - 1) % cuts) for i in range(cuts)],
-    )
+    sent, own = pl.pallas_call(
+        opening_kernel,
+        out_shape=(pltpu.VMEM((2, sites), jnp.float32), pltpu.VMEM((1, sites), jnp.float32)),
+        in_specs=[pl.BlockSpec(memory_space=pl.ANY)] * 3,
+        out_specs=(vmem, vmem),
+        scratch_shapes=[pltpu.VMEM((3, 1, sites), jnp.float32), pltpu.SemaphoreType.DMA((3,))],
+        compiler_params=pltpu.CompilerParams(vmem_limit_bytes=1024 * 1024),
+        cost_estimate=pl.CostEstimate(flops=8 * rows * sites * sites, bytes_accessed=8 * rows * sites, transcendentals=0),
+        name="opening",
+    )(*(pltpu.with_memory_space_constraint(x, pltpu.HBM) for x in (field, momenta, start_force)))
+    nxt = lax.ppermute(sent, CUTS, [(i, (i - 1) % cuts) for i in range(cuts)])
     diag, part = pl.pallas_call(
         diagonal_kernel,
         out_shape=(
             jax.ShapeDtypeStruct((rows // LANES, LANES), jnp.float32),
-            jax.ShapeDtypeStruct((devices, LANES), jnp.float32),
+            pltpu.VMEM((devices, LANES), jnp.float32),
         ),
-        in_specs=[vmem] * 8,
+        in_specs=[vmem] * 6,
         out_specs=(vmem, vmem),
         scratch_shapes=[
             pltpu.VMEM((2, sites, COLUMNS), jnp.bfloat16),
@@ -133,7 +153,7 @@
             flops=2 * rows * sites * sites, bytes_accessed=8 * rows * sites, transcendentals=2 * sites
         ),
         name="diagonal",
-    )(*map(held, (nxt, field, momenta, start_force, near, far, forward_prop, back_prop)))
+    )(*map(held, (nxt, own, near, far, forward_prop, back_prop)))
     straight = lax.ppermute(diag, ALL, [(i, (i + 2) % devices) for i in range(devices)])
     crossed = lax.ppermute(diag, ALL, [(i, ((i + 2) % devices) ^ 1) for i in range(devices)])
     parts = lax.all_to_all(part, ALL, split_axis=0, concat_axis=0, tiled=True)

time: 57.5 us -> 48.8 us (0.85)
  local copies, waits for them, and re-layouts: 8.67 us -> 0.03 us
  Pallas kernels: 10.9 us -> 12 us
  other arithmetic: 0.77 us -> 0 us
    unnamed x18 -> x12, local copies, waits for them, and re-layouts: 8.67 us -> 0.03 us
    pallas_call x0 -> x1, Pallas kernels: none -> 1.09 us  [on_device(): pl.pallas_call(opening_kernel, out_shape=(pltpu.VMEM((2, sites), jnp.floa...]
    add x1 -> x0, other arithmetic: 0.75 us -> none  [stepped(): return (field + stepsize * half, half)]
  transfers between devices with their start and end apart: 5 -> 5, of which waited for: 4 -> 4; matrix products, arithmetic and copies ran while one was open for 1% -> 0% of each run, Pallas kernels for 0% -> 2%
where the time goes in v2:
time: 48.8 us; the launch traced here: 48.6 us
  starting transfers between devices  25.3 us (52%)
  Pallas kernels  12 us (25%)
  waiting for transfers between devices  9.89 us (20%)
  between operations  1.36 us (3%)
    all_to_all x1, starting transfers between devices, on_device(): parts = lax.all_to_all(part, ALL, split_axis=0, concat_axis=0, tiled=True)  10.2 us
    pallas_call x1, Pallas kernels, on_device(): pl.pallas_call(diagonal_kernel, out_shape=(jax.ShapeDtypeStruct((rows //...  10.2 us
    ppermute x1, starting transfers between devices, on_device(): nxt = lax.ppermute(sent, CUTS, [(i, (i - 1) % cuts) for i in range(cuts)])  8.64 us
    ppermute x1, waiting for transfers between devices, on_device(): lax.ppermute(diag, ALL, [(i, (i + 2) % devices) for i in range(devices)])  6.94 us
    ppermute x1, starting transfers between devices, on_device(): far = lax.ppermute(near, 'site', [(0, 1), (1, 0)])  3.29 us
    ppermute x1, starting transfers between devices, on_device(): lax.ppermute(diag, ALL, [(i, (i + 2) % devices ^ 1) for i in range(device...  1.74 us
    all_to_all x1, waiting for transfers between devices, on_device(): parts = lax.all_to_all(part, ALL, split_axis=0, concat_axis=0, tiled=True)  1.47 us
    ppermute x1, starting transfers between devices, on_device(): lax.ppermute(diag, ALL, [(i, (i + 2) % devices) for i in range(devices)])  1.43 us
  transfers between devices with their start and end apart: 5, of which 4 were waited for; matrix products, arithmetic and copies ran while one was open for 0% of the time, Pallas kernels for 2%

profile of v2, /device:TPU:1, one launch (start us, length us, event | category | flops | bytes accessed | tf_op | source)
XLA Modules:
  0.0 48.6 jit_solution(1851950887891408389)
XLA Ops:
  0.6 0.0 copy-start.3
  0.6 0.0 copy-start.4
  0.7 0.0 copy-start.5
  0.7 3.3 %collective-permute-start.1 = (bf16[1024,2048]{1,0:T(8,128)(2,1)}, bf16[1024,2048]{1,0:T(8,128)(2,1)S(1)}, u32[]{:S(2)}, u32[]{:S(2)}) collective-permute-start(bf16[1024,2048]{1,0:T(8,128)(2,1)} %bitcast.6), channel_id=1, source_target_pairs={{0,1},{1,0},{2,3},{3,2},{4,5},{5,4},{6,7},{7,6},{8,9},{9,8},{10,11... | collective-permute-start | bytes 12582920 | tf_op jit(solution)/shard_map/ppermute | solution.py:127
  3.9 1.1 %opening.1 = (f32[2,2048]{1,0:T(2,128)S(1)}, f32[1,2048]{1,0:T(1,128)S(1)}) custom-call(f32[1,2048]{1,0:T(1,128)} %refs_1_.1, f32[1,2048]{1,0:T(1,128)} %refs_2_.1, f32[1,2048]{1,0:T(1,128)} %refs_3_.1), custom_call_target="tpu_custom_call" | custom-call | flops 34359738368 | bytes 16777216 | tf_op jit(solution)/shard_map/opening/pallas_call | solution.py:128
  5.0 8.6 %collective-permute-start = (f32[2,2048]{1,0:T(2,128)S(1)}, f32[2,2048]{1,0:T(2,128)S(1)}, u32[]{:S(2)}, u32[]{:S(2)}) collective-permute-start(f32[2,2048]{1,0:T(2,128)S(1)} %get-tuple-element.8), channel_id=1, source_target_pairs={{0,254},{2,0},{4,2},{6,4},{8,6},{10,8},{12,10},{14,12},{16,14},{18... | collective-permute-start | bytes 49160 | tf_op jit(solution)/shard_map/ppermute | solution.py:138
  13.7 0.9 %collective-permute-done.nxt_ref = f32[2,2048]{1,0:T(2,128)S(1)} collective-permute-done((f32[2,2048]{1,0:T(2,128)S(1)}, f32[2,2048]{1,0:T(2,128)S(1)}, u32[]{:S(2)}, u32[]{:S(2)}) %collective-permute-start) | collective-permute-done | bytes 16416 | tf_op jit(solution)/shard_map/ppermute | solution.py:138
  14.6 0.0 collective-permute-done.1.far_ref
  14.6 0.0 copy-done.3
  14.6 0.0 copy-done.4
  14.6 0.0 copy-done.5
  14.6 0.0 copy-start
  14.6 0.0 copy-start.1
  14.6 0.0 copy-start.2
  14.6 10.2 %diagonal.1 = (f32[8,128]{1,0:T(8,128)S(1)}, f32[256,128]{1,0:T(8,128)}) custom-call(f32[2,2048]{1,0:T(2,128)S(1)} %collective-permute-done.nxt_ref, f32[1,2048]{1,0:T(1,128)S(1)} %get-tuple-element.9.own_ref, bf16[1024,2048]{1,0:T(8,128)(2,1)S(1)} %bitcast.7, bf16[1024,2048]{1,0:T(8,128)(2,1)S(1)} %collective-permute-done.1.far_ref, ...), custom_call_target="tpu_custom_call" | custom-call | flops 8589934592 | bytes 16777216 | tf_op jit(solution)/shard_map/diagonal/pallas_call | solution.py:139
  24.8 10.2 %all-to-all-start = ((f32[256,1,128]{2,1,0:T(1,128)}), f32[256,1,128]{2,1,0:T(1,128)S(1)}, u32[]{:S(2)}, u32[]{:S(2)}) async-start(f32[256,1,128]{2,1,0:T(1,128)} %bitcast.2), calls=%async_computation | async-start | bytes 262144 | tf_op jit(solution)/shard_map/all_to_all | solution.py:159
  35.1 1.4 %collective-permute-start.2 = (f32[8,128]{1,0:T(8,128)S(1)}, f32[8,128]{1,0:T(8,128)S(1)}, u32[]{:S(2)}, u32[]{:S(2)}) collective-permute-start(f32[8,128]{1,0:T(8,128)S(1)} %get-tuple-element.10), channel_id=1, source_target_pairs={{0,2},{1,3},{2,4},{3,5},{4,6},{5,7},{6,8},{7,9},{8,10},{9,11},{10,... | collective-permute-start | bytes 12296 | tf_op jit(solution)/shard_map/ppermute | solution.py:157
  36.5 1.7 %collective-permute-start.3 = (f32[8,128]{1,0:T(8,128)S(1)}, f32[8,128]{1,0:T(8,128)S(1)}, u32[]{:S(2)}, u32[]{:S(2)}) collective-permute-start(f32[8,128]{1,0:T(8,128)S(1)} %get-tuple-element.10), channel_id=1, source_target_pairs={{0,3},{1,2},{2,5},{3,4},{4,7},{5,6},{6,9},{7,8},{8,11},{9,10},{10,... | collective-permute-start | bytes 12296 | tf_op jit(solution)/shard_map/ppermute | solution.py:158
  38.9 6.9 %collective-permute-done.2.refs_4_ = f32[8,128]{1,0:T(8,128)S(1)} collective-permute-done((f32[8,128]{1,0:T(8,128)S(1)}, f32[8,128]{1,0:T(8,128)S(1)}, u32[]{:S(2)}, u32[]{:S(2)}) %collective-permute-start.2) | collective-permute-done | bytes 4128 | tf_op jit(solution)/shard_map/ppermute | solution.py:157
  45.8 0.6 %collective-permute-done.3.refs_5_ = f32[8,128]{1,0:T(8,128)S(1)} collective-permute-done((f32[8,128]{1,0:T(8,128)S(1)}, f32[8,128]{1,0:T(8,128)S(1)}, u32[]{:S(2)}, u32[]{:S(2)}) %collective-permute-start.3) | collective-permute-done | bytes 4128 | tf_op jit(solution)/shard_map/ppermute | solution.py:158
  46.5 1.5 %all-to-all-done = f32[256,1,128]{2,1,0:T(1,128)S(1)} async-done(((f32[256,1,128]{2,1,0:T(1,128)}), f32[256,1,128]{2,1,0:T(1,128)S(1)}, u32[]{:S(2)}, u32[]{:S(2)}) %all-to-all-start) | async-done | bytes 131104 | tf_op jit(solution)/shard_map/all_to_all | solution.py:159
  47.9 0.0 copy-done
  47.9 0.0 copy-done.1
  47.9 0.0 copy-done.2
  47.9 0.7 %closing.1 = (f32[1,2048]{1,0:T(1,128)}, f32[1,2048]{1,0:T(1,128)}, f32[1,2048]{1,0:T(1,128)}, f32[1]{0:T(128)}) custom-call(s32[1]{0:T(128)S(6)} %copy.12.refs_0_, f32[1,2048]{1,0:T(1,128)S(1)} %copy-done, f32[1,2048]{1,0:T(1,128)S(1)} %copy-done.1, f32[1,2048]{1,0:T(1,128)S(1)} %copy-done.2, f32[8,128]{1,0:T(8,128)S(1)} %collective-permute-done.2.refs_4_, ...), custom_call_target="tpu_custom_call" | custom-call | tf_op jit(solution)/shard_map/closing/pallas_call | solution.py:161
Async XLA Ops:
  0.6 13.9 %copy-start.3 = (bf16[1,1024,2048]{2,1,0:T(8,128)(2,1)S(1)}, bf16[1,1024,2048]{2,1,0:T(8,128)(2,1)}, u32[]{:S(2)}) copy-start(bf16[1,1024,2048]{2,1,0:T(8,128)(2,1)} %param.10) | copy-start | bytes 12582916
  0.6 13.9 %copy-start.4 = (bf16[1024,2048]{1,0:T(8,128)(2,1)S(1)}, bf16[1024,2048]{1,0:T(8,128)(2,1)}, u32[]{:S(2)}) copy-start(bf16[1024,2048]{1,0:T(8,128)(2,1)} %forward_ref.1) | copy-start | bytes 12582916
  0.7 13.9 %copy-start.5 = (bf16[1024,2048]{1,0:T(8,128)(2,1)S(1)}, bf16[1024,2048]{1,0:T(8,128)(2,1)}, u32[]{:S(2)}) copy-start(bf16[1024,2048]{1,0:T(8,128)(2,1)} %back_ref.1) | copy-start | bytes 12582916
  0.7 13.9 %collective-permute-start.1 = (bf16[1024,2048]{1,0:T(8,128)(2,1)}, bf16[1024,2048]{1,0:T(8,128)(2,1)S(1)}, u32[]{:S(2)}, u32[]{:S(2)}) collective-permute-start(bf16[1024,2048]{1,0:T(8,128)(2,1)} %bitcast.6), channel_id=1, source_target_pairs={{0,1},{1,0},{2,3},{3,2},{4,5},{5,4},{6,7},{7,6},{8,9},{9,8},{10,11... | collective-permute-start | bytes 12582920 | tf_op jit(solution)/shard_map/ppermute | solution.py:127
  5.0 9.5 %collective-permute-start = (f32[2,2048]{1,0:T(2,128)S(1)}, f32[2,2048]{1,0:T(2,128)S(1)}, u32[]{:S(2)}, u32[]{:S(2)}) collective-permute-start(f32[2,2048]{1,0:T(2,128)S(1)} %get-tuple-element.8), channel_id=1, source_target_pairs={{0,254},{2,0},{4,2},{6,4},{8,6},{10,8},{12,10},{14,12},{16,14},{18... | collective-permute-start | bytes 49160 | tf_op jit(solution)/shard_map/ppermute | solution.py:138
  14.6 33.4 %copy-start = (f32[1,2048]{1,0:T(1,128)S(1)}, f32[1,2048]{1,0:T(1,128)}, u32[]{:S(2)}) copy-start(f32[1,2048]{1,0:T(1,128)} %refs_1_.1) | copy-start | bytes 24580
  14.6 33.3 %copy-start.1 = (f32[1,2048]{1,0:T(1,128)S(1)}, f32[1,2048]{1,0:T(1,128)}, u32[]{:S(2)}) copy-start(f32[1,2048]{1,0:T(1,128)} %refs_2_.1) | copy-start | bytes 24580
  14.6 33.3 %copy-start.2 = (f32[1,2048]{1,0:T(1,128)S(1)}, f32[1,2048]{1,0:T(1,128)}, u32[]{:S(2)}) copy-start(f32[1,2048]{1,0:T(1,128)} %refs_3_.1) | copy-start | bytes 24580
  24.8 23.1 %all-to-all-start = ((f32[256,1,128]{2,1,0:T(1,128)}), f32[256,1,128]{2,1,0:T(1,128)S(1)}, u32[]{:S(2)}, u32[]{:S(2)}) async-start(f32[256,1,128]{2,1,0:T(1,128)} %bitcast.2), calls=%async_computation | async-start | bytes 262144 | tf_op jit(solution)/shard_map/all_to_all | solution.py:159
  35.1 10.8 %collective-permute-start.2 = (f32[8,128]{1,0:T(8,128)S(1)}, f32[8,128]{1,0:T(8,128)S(1)}, u32[]{:S(2)}, u32[]{:S(2)}) collective-permute-start(f32[8,128]{1,0:T(8,128)S(1)} %get-tuple-element.10), channel_id=1, source_target_pairs={{0,2},{1,3},{2,4},{3,5},{4,6},{5,7},{6,8},{7,9},{8,10},{9,11},{10,... | collective-permute-start | bytes 12296 | tf_op jit(solution)/shard_map/ppermute | solution.py:157
  36.5 10.0 %collective-permute-start.3 = (f32[8,128]{1,0:T(8,128)S(1)}, f32[8,128]{1,0:T(8,128)S(1)}, u32[]{:S(2)}, u32[]{:S(2)}) collective-permute-start(f32[8,128]{1,0:T(8,128)S(1)} %get-tuple-element.10), channel_id=1, source_target_pairs={{0,3},{1,2},{2,5},{3,4},{4,7},{5,6},{6,9},{7,8},{8,11},{9,10},{10,... | collective-permute-start | bytes 12296 | tf_op jit(solution)/shard_map/ppermute | solution.py:158

commit v3 on v2

--- a/solution.py
+++ b/solution.py
@@ -25,7 +25,7 @@
     return force, half - 0.5 * stepsize * force
 
 
-def opening_kernel(field_ref, momenta_ref, start_ref, sent_ref, own_ref, held, sems):
+def opening_kernel(field_ref, momenta_ref, start_ref, own_ref, held, sems):
     copies = [
         pltpu.make_async_copy(ref, held.at[k], sems.at[k])
         for k, ref in enumerate((field_ref, momenta_ref, start_ref))
@@ -35,9 +35,7 @@
     for copy in copies:
         copy.wait()
     field, momenta = held[0], held[1]
-    trial, half = stepped(field, momenta, held[2])
-    sent_ref[0:1, :] = trial
-    sent_ref[1:2, :] = half
+    trial = stepped(field, momenta, held[2])[0]
     own_ref[...] = trial * trial - momenta * momenta - field * field
 
 
@@ -53,6 +51,7 @@
         own = jnp.where(first, whole[:blocks], whole[blocks:])
         return own, jnp.where(first, whole[blocks:], whole[:blocks])
 
+    base = 0.5 * jnp.sum(own_ref[...])
     growth = jnp.exp(coupling * nxt_ref[0:1, :])
     factors = jnp.transpose(jnp.concatenate(by_rows(growth), axis=0))
     near_at = pl.multiple_of(site * rows, LANES)
@@ -92,7 +91,7 @@
     )
     diag_ref[...] = diag
     moved = moved_by(by_rows(nxt_ref[0:1, :])[0], by_rows(nxt_ref[1:2, :])[0], diag)[1]
-    total = jnp.sum(moved * moved) + 0.5 * jnp.sum(own_ref[...])
+    total = jnp.sum(moved * moved) + base
     part_ref[...] = jnp.full(part_ref.shape, total, jnp.float32)
 
 
@@ -124,18 +123,19 @@
     def held(x):
         return pltpu.with_memory_space_constraint(x, pltpu.VMEM)
 
+    sent = jnp.concatenate(stepped(field, momenta, start_force), axis=0)
+    nxt = lax.ppermute(sent, ALL, [(i, ((i - 2) % devices) ^ 1) for i in range(devices)])
     far = lax.ppermute(near, "site", [(0, 1), (1, 0)])
-    sent, own = pl.pallas_call(
+    own = pl.pallas_call(
         opening_kernel,
-        out_shape=(pltpu.VMEM((2, sites), jnp.float32), pltpu.VMEM((1, sites), jnp.float32)),
+        out_shape=pltpu.VMEM((1, sites), jnp.float32),
         in_specs=[pl.BlockSpec(memory_space=pl.ANY)] * 3,
-        out_specs=(vmem, vmem),
+        out_specs=vmem,
         scratch_shapes=[pltpu.VMEM((3, 1, sites), jnp.float32), pltpu.SemaphoreType.DMA((3,))],
         compiler_params=pltpu.CompilerParams(vmem_limit_bytes=1024 * 1024),
         cost_estimate=pl.CostEstimate(flops=8 * rows * sites * sites, bytes_accessed=8 * rows * sites, transcendentals=0),
         name="opening",
     )(*(pltpu.with_memory_space_constraint(x, pltpu.HBM) for x in (field, momenta, start_force)))
-    nxt = lax.ppermute(sent, CUTS, [(i, (i - 1) % cuts) for i in range(cuts)])
     diag, part = pl.pallas_call(
         diagonal_kernel,
         out_shape=(

time: 48.8 us -> 48.3 us (0.990)
  waiting for transfers between devices: 9.89 us -> 9.09 us
  other arithmetic: 0 us -> 0.77 us
    ppermute x1, waiting for transfers between devices: 0.87 us -> 0.06 us  [on_device(): lax.ppermute(sent, ALL, [(i, (i - 2) % devices ^ 1) for i in range(device...]
    add x0 -> x1, other arithmetic: none -> 0.75 us  [stepped(): return (field + stepsize * half, half)]
  transfers between devices with their start and end apart: 5 -> 5, of which waited for: 4 -> 4; matrix products, arithmetic and copies ran while one was open for 0% -> 2% of each run, Pallas kernels for 2% -> 2%
where the time goes in v3:
time: 48.3 us; the launch traced here: 48 us
  starting transfers between devices  25.1 us (52%)
  Pallas kernels  11.6 us (24%)
  waiting for transfers between devices  9.09 us (19%)
  between operations  1.37 us (3%)
  other arithmetic  0.77 us (2%)
    pallas_call x1, Pallas kernels, on_device(): pl.pallas_call(diagonal_kernel, out_shape=(jax.ShapeDtypeStruct((rows //...  10.2 us
    all_to_all x1, starting transfers between devices, on_device(): parts = lax.all_to_all(part, ALL, split_axis=0, concat_axis=0, tiled=True)  10.1 us
    ppermute x1, starting transfers between devices, on_device(): lax.ppermute(sent, ALL, [(i, (i - 2) % devices ^ 1) for i in range(device...  8.49 us
    ppermute x1, waiting for transfers between devices, on_device(): lax.ppermute(diag, ALL, [(i, (i + 2) % devices) for i in range(devices)])  6.94 us
    ppermute x1, starting transfers between devices, on_device(): far = lax.ppermute(near, 'site', [(0, 1), (1, 0)])  3.29 us
    ppermute x1, starting transfers between devices, on_device(): lax.ppermute(diag, ALL, [(i, (i + 2) % devices ^ 1) for i in range(device...  1.74 us
    all_to_all x1, waiting for transfers between devices, on_device(): parts = lax.all_to_all(part, ALL, split_axis=0, concat_axis=0, tiled=True)  1.47 us
    ppermute x1, starting transfers between devices, on_device(): lax.ppermute(diag, ALL, [(i, (i + 2) % devices) for i in range(devices)])  1.43 us
  transfers between devices with their start and end apart: 5, of which 4 were waited for; matrix products, arithmetic and copies ran while one was open for 2% of the time, Pallas kernels for 2%

profile of v3, /device:TPU:1, one launch (start us, length us, event | category | flops | bytes accessed | tf_op | source)
XLA Modules:
  0.0 48.0 jit_solution(13279402799251261060)
XLA Ops:
  0.6 3.3 %collective-permute-start.1 = (bf16[1024,2048]{1,0:T(8,128)(2,1)}, bf16[1024,2048]{1,0:T(8,128)(2,1)S(1)}, u32[]{:S(2)}, u32[]{:S(2)}) collective-permute-start(bf16[1024,2048]{1,0:T(8,128)(2,1)} %bitcast.6), channel_id=1, source_target_pairs={{0,1},{1,0},{2,3},{3,2},{4,5},{5,4},{6,7},{7,6},{8,9},{9,8},{10,11... | collective-permute-start | bytes 12582920 | tf_op jit(solution)/shard_map/ppermute | solution.py:128
  3.9 0.8 %multiply_add_fusion = (f32[1,2048]{1,0:T(1,128)S(1)}, f32[1,2048]{1,0:T(1,128)S(1)}) fusion(f32[1,2048]{1,0:T(1,128)} %refs_1_.1, f32[1,2048]{1,0:T(1,128)} %refs_2_.1, f32[1,2048]{1,0:T(1,128)} %refs_3_.1), kind=kLoop, calls=%fused_computation.1 | loop fusion | flops 8192 | bytes 40960 | tf_op jit(solution)/shard_map/add | solution.py:20
  4.7 0.0 copy-start.3
  4.7 0.0 copy-start.4
  4.7 0.0 copy-start.5
  4.7 8.5 %collective-permute-start = (f32[2,2048]{1,0:T(2,128)S(1)}, f32[2,2048]{1,0:T(2,128)S(1)}, u32[]{:S(2)}, u32[]{:S(2)}) collective-permute-start(f32[2,2048]{1,0:T(2,128)S(1)} %pad_maximum_fusion), channel_id=1, source_target_pairs={{0,255},{1,254},{2,1},{3,0},{4,3},{5,2},{6,5},{7,4},{8,7},{9,6},{1... | collective-permute-start | bytes 49160 | tf_op jit(solution)/shard_map/ppermute | solution.py:127
  13.2 0.8 %opening.1.own_ref = f32[1,2048]{1,0:T(1,128)S(1)} custom-call(f32[1,2048]{1,0:T(1,128)} %refs_1_.1, f32[1,2048]{1,0:T(1,128)} %refs_2_.1, f32[1,2048]{1,0:T(1,128)} %refs_3_.1), custom_call_target="tpu_custom_call" | custom-call | flops 34359738368 | bytes 16777216 | tf_op jit(solution)/shard_map/opening/pallas_call | solution.py:129
  14.0 0.0 copy-start
  14.0 0.0 copy-start.1
  14.0 0.0 copy-start.2
  14.0 0.1 collective-permute-done.nxt_ref
  14.1 0.0 collective-permute-done.1.far_ref
  14.1 0.0 copy-done.3
  14.1 0.0 copy-done.4
  14.1 0.0 copy-done.5
  14.1 10.2 %diagonal.1 = (f32[8,128]{1,0:T(8,128)S(1)}, f32[256,128]{1,0:T(8,128)}) custom-call(f32[2,2048]{1,0:T(2,128)S(1)} %collective-permute-done.nxt_ref, f32[1,2048]{1,0:T(1,128)S(1)} %opening.1.own_ref, bf16[1024,2048]{1,0:T(8,128)(2,1)S(1)} %bitcast.7, bf16[1024,2048]{1,0:T(8,128)(2,1)S(1)} %collective-permute-done.1.far_ref, ...), custom_call_target="tpu_custom_call" | custom-call | flops 8589934592 | bytes 16777216 | tf_op jit(solution)/shard_map/diagonal/pallas_call | solution.py:139
  24.3 10.1 %all-to-all-start = ((f32[256,1,128]{2,1,0:T(1,128)}), f32[256,1,128]{2,1,0:T(1,128)S(1)}, u32[]{:S(2)}, u32[]{:S(2)}) async-start(f32[256,1,128]{2,1,0:T(1,128)} %bitcast.2), calls=%async_computation | async-start | bytes 262144 | tf_op jit(solution)/shard_map/all_to_all | solution.py:159
  34.4 1.4 %collective-permute-start.2 = (f32[8,128]{1,0:T(8,128)S(1)}, f32[8,128]{1,0:T(8,128)S(1)}, u32[]{:S(2)}, u32[]{:S(2)}) collective-permute-start(f32[8,128]{1,0:T(8,128)S(1)} %get-tuple-element.6), channel_id=1, source_target_pairs={{0,2},{1,3},{2,4},{3,5},{4,6},{5,7},{6,8},{7,9},{8,10},{9,11},{10,... | collective-permute-start | bytes 12296 | tf_op jit(solution)/shard_map/ppermute | solution.py:157
  35.9 1.7 %collective-permute-start.3 = (f32[8,128]{1,0:T(8,128)S(1)}, f32[8,128]{1,0:T(8,128)S(1)}, u32[]{:S(2)}, u32[]{:S(2)}) collective-permute-start(f32[8,128]{1,0:T(8,128)S(1)} %get-tuple-element.6), channel_id=1, source_target_pairs={{0,3},{1,2},{2,5},{3,4},{4,7},{5,6},{6,9},{7,8},{8,11},{9,10},{10,... | collective-permute-start | bytes 12296 | tf_op jit(solution)/shard_map/ppermute | solution.py:158
  38.3 6.9 %collective-permute-done.2.refs_4_ = f32[8,128]{1,0:T(8,128)S(1)} collective-permute-done((f32[8,128]{1,0:T(8,128)S(1)}, f32[8,128]{1,0:T(8,128)S(1)}, u32[]{:S(2)}, u32[]{:S(2)}) %collective-permute-start.2) | collective-permute-done | bytes 4128 | tf_op jit(solution)/shard_map/ppermute | solution.py:157
  45.2 0.6 %collective-permute-done.3.refs_5_ = f32[8,128]{1,0:T(8,128)S(1)} collective-permute-done((f32[8,128]{1,0:T(8,128)S(1)}, f32[8,128]{1,0:T(8,128)S(1)}, u32[]{:S(2)}, u32[]{:S(2)}) %collective-permute-start.3) | collective-permute-done | bytes 4128 | tf_op jit(solution)/shard_map/ppermute | solution.py:158
  45.8 1.5 %all-to-all-done = f32[256,1,128]{2,1,0:T(1,128)S(1)} async-done(((f32[256,1,128]{2,1,0:T(1,128)}), f32[256,1,128]{2,1,0:T(1,128)S(1)}, u32[]{:S(2)}, u32[]{:S(2)}) %all-to-all-start) | async-done | bytes 131104 | tf_op jit(solution)/shard_map/all_to_all | solution.py:159
  47.3 0.0 copy-done
  47.3 0.0 copy-done.1
  47.3 0.0 copy-done.2
  47.3 0.7 %closing.1 = (f32[1,2048]{1,0:T(1,128)}, f32[1,2048]{1,0:T(1,128)}, f32[1,2048]{1,0:T(1,128)}, f32[1]{0:T(128)}) custom-call(s32[1]{0:T(128)S(6)} %copy.12.refs_0_, f32[1,2048]{1,0:T(1,128)S(1)} %copy-done, f32[1,2048]{1,0:T(1,128)S(1)} %copy-done.1, f32[1,2048]{1,0:T(1,128)S(1)} %copy-done.2, f32[8,128]{1,0:T(8,128)S(1)} %collective-permute-done.2.refs_4_, ...), custom_call_target="tpu_custom_call" | custom-call | tf_op jit(solution)/shard_map/closing/pallas_call | solution.py:161
  (1 shorter events, 0.0 us)
Async XLA Ops:
  0.6 13.5 %collective-permute-start.1 = (bf16[1024,2048]{1,0:T(8,128)(2,1)}, bf16[1024,2048]{1,0:T(8,128)(2,1)S(1)}, u32[]{:S(2)}, u32[]{:S(2)}) collective-permute-start(bf16[1024,2048]{1,0:T(8,128)(2,1)} %bitcast.6), channel_id=1, source_target_pairs={{0,1},{1,0},{2,3},{3,2},{4,5},{5,4},{6,7},{7,6},{8,9},{9,8},{10,11... | collective-permute-start | bytes 12582920 | tf_op jit(solution)/shard_map/ppermute | solution.py:128
  4.7 9.4 %copy-start.3 = (bf16[1,1024,2048]{2,1,0:T(8,128)(2,1)S(1)}, bf16[1,1024,2048]{2,1,0:T(8,128)(2,1)}, u32[]{:S(2)}) copy-start(bf16[1,1024,2048]{2,1,0:T(8,128)(2,1)} %param.10) | copy-start | bytes 12582916
  4.7 9.4 %copy-start.4 = (bf16[1024,2048]{1,0:T(8,128)(2,1)S(1)}, bf16[1024,2048]{1,0:T(8,128)(2,1)}, u32[]{:S(2)}) copy-start(bf16[1024,2048]{1,0:T(8,128)(2,1)} %forward_ref.1) | copy-start | bytes 12582916
  4.7 9.4 %copy-start.5 = (bf16[1024,2048]{1,0:T(8,128)(2,1)S(1)}, bf16[1024,2048]{1,0:T(8,128)(2,1)}, u32[]{:S(2)}) copy-start(bf16[1024,2048]{1,0:T(8,128)(2,1)} %back_ref.1) | copy-start | bytes 12582916
  4.7 9.4 %collective-permute-start = (f32[2,2048]{1,0:T(2,128)S(1)}, f32[2,2048]{1,0:T(2,128)S(1)}, u32[]{:S(2)}, u32[]{:S(2)}) collective-permute-start(f32[2,2048]{1,0:T(2,128)S(1)} %pad_maximum_fusion), channel_id=1, source_target_pairs={{0,255},{1,254},{2,1},{3,0},{4,3},{5,2},{6,5},{7,4},{8,7},{9,6},{1... | collective-permute-start | bytes 49160 | tf_op jit(solution)/shard_map/ppermute | solution.py:127
  14.0 33.3 %copy-start = (f32[1,2048]{1,0:T(1,128)S(1)}, f32[1,2048]{1,0:T(1,128)}, u32[]{:S(2)}) copy-start(f32[1,2048]{1,0:T(1,128)} %refs_1_.1) | copy-start | bytes 24580
  14.0 33.3 %copy-start.1 = (f32[1,2048]{1,0:T(1,128)S(1)}, f32[1,2048]{1,0:T(1,128)}, u32[]{:S(2)}) copy-start(f32[1,2048]{1,0:T(1,128)} %refs_2_.1) | copy-start | bytes 24580
  14.0 33.3 %copy-start.2 = (f32[1,2048]{1,0:T(1,128)S(1)}, f32[1,2048]{1,0:T(1,128)}, u32[]{:S(2)}) copy-start(f32[1,2048]{1,0:T(1,128)} %refs_3_.1) | copy-start | bytes 24580
  24.3 23.0 %all-to-all-start = ((f32[256,1,128]{2,1,0:T(1,128)}), f32[256,1,128]{2,1,0:T(1,128)S(1)}, u32[]{:S(2)}, u32[]{:S(2)}) async-start(f32[256,1,128]{2,1,0:T(1,128)} %bitcast.2), calls=%async_computation | async-start | bytes 262144 | tf_op jit(solution)/shard_map/all_to_all | solution.py:159
  34.4 10.8 %collective-permute-start.2 = (f32[8,128]{1,0:T(8,128)S(1)}, f32[8,128]{1,0:T(8,128)S(1)}, u32[]{:S(2)}, u32[]{:S(2)}) collective-permute-start(f32[8,128]{1,0:T(8,128)S(1)} %get-tuple-element.6), channel_id=1, source_target_pairs={{0,2},{1,3},{2,4},{3,5},{4,6},{5,7},{6,8},{7,9},{8,10},{9,11},{10,... | collective-permute-start | bytes 12296 | tf_op jit(solution)/shard_map/ppermute | solution.py:157
  35.9 10.0 %collective-permute-start.3 = (f32[8,128]{1,0:T(8,128)S(1)}, f32[8,128]{1,0:T(8,128)S(1)}, u32[]{:S(2)}, u32[]{:S(2)}) collective-permute-start(f32[8,128]{1,0:T(8,128)S(1)} %get-tuple-element.6), channel_id=1, source_target_pairs={{0,3},{1,2},{2,5},{3,4},{4,7},{5,6},{6,9},{7,8},{8,11},{9,10},{10,... | collective-permute-start | bytes 12296 | tf_op jit(solution)/shard_map/ppermute | solution.py:158
